TPU v7x, 32 devices: a whole 2x2x4 slice. The times are simulated.
32 devices in a mesh: layer: 8 (over y, x, core), lat: 4 (over z).
Axes of the slice: x: 2, y: 2, z: 4, core: 2. Of those that a mesh axis runs over, the one named last changes fastest.
Arguments:
- activations: bfloat16 [1536, 4096], P('layer', 'lat'), may hold values from -6 to 6
- w_enc: bfloat16 [1536, 8192], P('layer', 'lat'), may hold values from -0.15625 to 0.15625
- w_dec: bfloat16 [1536, 8192], P('layer', 'lat'), may hold values from -0.25 to 0.25
- b_enc: bfloat16 [8192], P('lat'), may hold values from -3 to 3
- b_dec: float32 [1536], P('layer'), may hold values from -3 to 3
- tile_ids: int32 [4, 4], replicated, may hold values from -1 to 63, as said below
Outputs:
- d_w_enc: bfloat16 [1536, 8192], P('layer', 'lat')
- d_w_dec: bfloat16 [1536, 8192], P('layer', 'lat')
- d_b_enc: float32 [8192], P('lat')
Inputs may be any that keep to these rules, and one draw needn't show every extreme that they name: `tile_ids`: row b lists the tiles of block b: live ids first, then -1. Live ids of a row are distinct, and no two of them share an owner id // 16. Each row has at least half of 4 (rounded up) live slots; some row has 4. One owner is named in every row.
All inputs are finite; a program needn't handle non-finite values.
Results may differ from a plain program's by a relative error of at most 0.02.
The roundings to bfloat16 on the way count: a program that leaves them out, or rounds other values in their place, can miss the bound.
Values may be sent and summed in bfloat16 or wider, within the bound.
No kernel may reach another device: no remote copies, remote signals or barrier semaphores. Data moves between devices by JAX's collectives and lax.ppermute only.
A program may use at most 64 MiB of HBM per device.

v0:
```python
import math
import jax
import jax.numpy as jnp
from jax import lax
from jax.sharding import PartitionSpec as P

TILE = 128


def rounded(value):
    return lax.optimization_barrier(value.astype(jnp.bfloat16)).astype(jnp.float32)


def local(activations, w_enc, w_dec, b_enc, b_dec, tile_ids):
    feature_count, row_count = activations.shape
    latent_count = w_enc.shape[1]
    owner_count = lax.axis_size("lat")
    tile_count = latent_count // TILE
    position = lax.axis_index("lat")
    owner_ids = jnp.where(tile_ids >= 0, tile_ids // tile_count, -1)
    matched = owner_ids == position
    local_tile = jnp.sum(jnp.where(matched, tile_ids % tile_count, 0), axis=1)
    wanted = jnp.any(matched, axis=1)
    chosen = (local_tile[:, None] == jnp.arange(tile_count)[None, :]) & wanted[:, None]
    chosen_half = chosen.astype(jnp.bfloat16)
    enc_table = w_enc.reshape(feature_count, tile_count, TILE)
    dec_table = w_dec.reshape(feature_count, tile_count, TILE)
    bias_table = b_enc.reshape(tile_count, TILE)
    enc_send = jnp.einsum(
        "rt,ftc->rfc", chosen_half, enc_table, preferred_element_type=jnp.float32
    ).astype(jnp.bfloat16)
    dec_send = jnp.einsum(
        "rt,ftc->rfc", chosen_half, dec_table, preferred_element_type=jnp.float32
    ).astype(jnp.bfloat16)
    bias_send = jnp.dot(chosen_half, bias_table, preferred_element_type=jnp.float32).astype(
        jnp.bfloat16
    )
    enc_recv, dec_recv, bias_recv = (
        lax.all_to_all(enc_send, "lat", split_axis=0, concat_axis=0, tiled=True),
        lax.all_to_all(dec_send, "lat", split_axis=0, concat_axis=0, tiled=True),
        lax.all_to_all(bias_send, "lat", split_axis=0, concat_axis=0, tiled=True),
    )
    my_list = lax.dynamic_index_in_dim(tile_ids, position, 0, keepdims=False)
    live_slot = my_list >= 0
    source = jnp.where(live_slot, my_list // tile_count, 0)
    live_half = live_slot.astype(jnp.bfloat16)
    live_float = live_slot.astype(jnp.float32)
    enc_cols = jnp.take(enc_recv, source, axis=0) * live_half[:, None, None]
    bias_cols = jnp.take(bias_recv, source, axis=0).astype(jnp.float32)
    partial_value = rounded(
        jnp.einsum("fr,kfc->rkc", activations, enc_cols, preferred_element_type=jnp.float32)
    )
    preact = lax.psum(partial_value, "layer") + bias_cols[None]
    latent_codes = (jax.nn.relu(preact) * live_float[None, :, None]).astype(jnp.bfloat16)
    dec_cols = jnp.take(dec_recv, source, axis=0) * live_half[:, None, None]
    rebuilt = (
        jnp.einsum("rkc,kfc->fr", latent_codes, dec_cols, preferred_element_type=jnp.float32)
        + b_dec[:, None]
    )
    residual = rebuilt - activations.astype(jnp.float32)
    grad_err = (residual / math.sqrt(row_count)).astype(jnp.bfloat16)
    dec_grad = jnp.einsum(
        "fr,rkc->kfc", grad_err, latent_codes, preferred_element_type=jnp.float32
    ).astype(jnp.bfloat16)
    back_part = rounded(
        jnp.einsum("fr,kfc->rkc", grad_err, dec_cols, preferred_element_type=jnp.float32)
    )
    grad_total = lax.psum(back_part, "layer")
    code_grad = (grad_total * (latent_codes > 0)).astype(jnp.bfloat16)
    enc_grad = jnp.einsum(
        "fr,rkc->kfc", activations, code_grad, preferred_element_type=jnp.float32
    ).astype(jnp.bfloat16)
    bias_grad = jnp.sum(code_grad, axis=0, dtype=jnp.float32).astype(jnp.bfloat16)
    placement = ((source[:, None] == jnp.arange(owner_count)[None, :]) & live_slot[:, None]).astype(
        jnp.bfloat16
    )
    enc_return = jnp.einsum(
        "ko,kfc->ofc", placement, enc_grad, preferred_element_type=jnp.float32
    ).astype(jnp.bfloat16)
    dec_return = jnp.einsum(
        "ko,kfc->ofc", placement, dec_grad, preferred_element_type=jnp.float32
    ).astype(jnp.bfloat16)
    bias_return = jnp.einsum(
        "ko,kc->oc", placement, bias_grad, preferred_element_type=jnp.float32
    ).astype(jnp.bfloat16)
    enc_got, dec_got, bias_got = (
        lax.all_to_all(enc_return, "lat", split_axis=0, concat_axis=0, tiled=True),
        lax.all_to_all(dec_return, "lat", split_axis=0, concat_axis=0, tiled=True),
        lax.all_to_all(bias_return, "lat", split_axis=0, concat_axis=0, tiled=True),
    )
    d_w_enc = (
        jnp.einsum("rt,rfc->ftc", chosen_half, enc_got, preferred_element_type=jnp.float32)
        .reshape(feature_count, latent_count)
        .astype(jnp.bfloat16)
    )
    d_w_dec = (
        jnp.einsum("rt,rfc->ftc", chosen_half, dec_got, preferred_element_type=jnp.float32)
        .reshape(feature_count, latent_count)
        .astype(jnp.bfloat16)
    )
    d_b_enc = jnp.einsum(
        "rt,rc->tc", chosen_half, bias_got, preferred_element_type=jnp.float32
    ).reshape(latent_count)
    return (d_w_enc, d_w_dec, d_b_enc)


def solution(mesh):
    return jax.shard_map(
        local,
        mesh=mesh,
        in_specs=(
            P("layer", "lat"),
            P("layer", "lat"),
            P("layer", "lat"),
            P("lat"),
            P("layer"),
            P(),
        ),
        out_specs=(P("layer", "lat"), P("layer", "lat"), P("lat")),
        check_vma=False,
    )
```

profile of v0, /device:TPU:0, one launch (start us, length us, event | category | flops | bytes accessed | tf_op | source)
XLA Modules:
  0.0 188.2 jit_solution(17841347270297134224)
XLA Ops:
  7.2 0.0 copy-start
  7.2 0.0 copy-start.2
  7.2 0.9 fusion.44
  8.1 0.8 fusion.23
  8.9 0.1 fusion.26
  9.0 0.0 copy-done
  9.0 0.1 fusion.8
  9.1 0.6 copy.46
  9.7 6.3 %all-to-all-start.1 = ((bf16[4,1,128]{2,1,0:T(2,128)(2,1)}), bf16[4,1,128]{2,1,0:T(2,128)(2,1)S(1)}, u32[]{:S(2)}, u32[]{:S(2)}) async-start(bf16[4,1,128]{2,1,0:T(2,128)(2,1)} %copy.46), calls=%async_computation.1 | async-start | bytes 4096 | tf_op jit(solution)/shard_map/all_to_all | solution.py:41
  16.0 0.7 fusion.42
  16.7 0.7 compare_and_fusion
  17.4 0.0 copy-start.6
  17.5 1.3 copy.65
  18.8 0.3 convolution_convert_fusion.7
  19.0 0.0 copy-done.2
  19.0 0.0 copy-start.4
  19.0 0.2 copy.66
  19.2 0.0 copy-done.12
  19.2 0.3 convolution_convert_fusion.6
  19.5 0.7 fusion.35
  20.2 0.7 copy.45
  20.9 0.7 copy.47
  21.6 0.0 all-to-all-done.1
  21.6 5.1 %all-to-all-start = ((bf16[4,192,128]{2,1,0:T(8,128)(2,1)}), bf16[4,192,128]{2,1,0:T(8,128)(2,1)S(1)}, u32[]{:S(2)}, u32[]{:S(2)}) async-start(bf16[4,192,128]{2,1,0:T(8,128)(2,1)} %copy.45), calls=%async_computation | async-start | bytes 393216 | tf_op jit(solution)/shard_map/all_to_all | solution.py:39
  26.7 0.6 gather_fusion
  27.3 0.1 select_convert_fusion.1
  27.3 6.6 %all-to-all-done = bf16[4,192,128]{2,1,0:T(8,128)(2,1)S(1)} async-done(((bf16[4,192,128]{2,1,0:T(8,128)(2,1)}), bf16[4,192,128]{2,1,0:T(8,128)(2,1)S(1)}, u32[]{:S(2)}, u32[]{:S(2)}) %all-to-all-start) | async-done | bytes 196640 | tf_op jit(solution)/shard_map/all_to_all | solution.py:39
  34.0 3.4 %all-to-all-start.2 = ((bf16[4,192,128]{2,1,0:T(8,128)(2,1)}), bf16[4,192,128]{2,1,0:T(8,128)(2,1)S(1)}, u32[]{:S(2)}, u32[]{:S(2)}) async-start(bf16[4,192,128]{2,1,0:T(8,128)(2,1)} %copy.47), calls=%async_computation.2 | async-start | bytes 393216 | tf_op jit(solution)/shard_map/all_to_all | solution.py:40
  37.3 0.0 all-reduce.3.cloned.1.call-start
  37.4 0.6 gather_fusion.1
  38.0 0.6 fusion
  38.6 56.5 %all-reduce.4 = f32[1024,4,128]{0,2,1:T(8,128)S(1)} all-reduce(bf16[1024,4,128]{0,2,1:T(8,128)(2,1)S(1)} %fusion), channel_id=1, replica_groups=mesh['layer'=8,'lat'=4] {'layer'}, use_global_device_ids=true, to_apply=%region_2.4 | all-reduce | flops 524288 | bytes 3145728 | tf_op jit(solution)/shard_map/psum | solution.py:53
  95.1 0.3 multiply_convert_fusion
  95.4 0.0 all-to-all-done.2
  95.4 1.2 gather_fusion.2
  96.7 1.6 fusion.5
  98.3 1.6 convolution_convert_fusion
  99.9 0.0 all-reduce.3.cloned.1.call-update
  99.9 0.5 fusion.7
  100.4 0.0 copy-start.11
  100.4 0.0 copy-start.13
  100.4 1.0 convolution_convert_fusion.8
  101.4 0.7 copy.56
  102.1 5.0 %all-to-all-start.4 = ((bf16[4,192,128]{2,1,0:T(8,128)(2,1)}), bf16[4,192,128]{2,1,0:T(8,128)(2,1)S(1)}, u32[]{:S(2)}, u32[]{:S(2)}) async-start(bf16[4,192,128]{2,1,0:T(8,128)(2,1)} %copy.56), calls=%async_computation.4 | async-start | bytes 393216 | tf_op jit(solution)/shard_map/all_to_all | solution.py:88
  107.1 49.9 %all-reduce.3.cloned.1.call-done = bf16[1024,4,128]{0,2,1:T(8,128)(2,1)} async-done(((bf16[1024,4,128]{0,2,1:T(8,128)(2,1)}), bf16[1024,4,128]{0,2,1:T(8,128)(2,1)}) %all-reduce.3.cloned.1.call-update) | async-done | bytes 1048592 | tf_op jit(solution)/shard_map/psum | solution.py:68
  156.9 0.0 copy-done.9
  157.0 2.0 %fusion.41 = bf16[4,128]{1,0:T(4,128)(2,1)S(1)} fusion(bf16[1024,4,128]{0,2,1:T(8,128)(2,1)} %all-reduce.3.cloned.1.call-done, f32[4]{0:T(128)S(1)} %copy-done.9, f32[1024,4,128]{0,2,1:T(8,128)S(1)} %all-reduce.4, f32[4,128]{1,0:T(4,128)S(1)} %select_convert_fusion.1), kind=kLoop, calls=%fused_computation.90 | loop fusion | flops 4718080 | bytes 3148816 | tf_op jit(solution)/shard_map/reduce_sum | solution.py:73
  158.9 0.0 copy-done.13
  158.9 0.1 fusion.9
  159.1 0.6 copy.58
  159.7 0.0 copy-done.5
  159.7 0.5 fusion.6
  160.2 0.0 all-to-all-done.4
  160.2 4.5 %all-to-all-start.5 = ((bf16[4,1,128]{2,1,0:T(2,128)(2,1)}), bf16[4,1,128]{2,1,0:T(2,128)(2,1)S(1)}, u32[]{:S(2)}, u32[]{:S(2)}) async-start(bf16[4,1,128]{2,1,0:T(2,128)(2,1)} %copy.58), calls=%async_computation.5 | async-start | bytes 4096 | tf_op jit(solution)/shard_map/all_to_all | solution.py:89
  164.7 0.3 convolution_convert_fusion.9
  165.0 0.7 copy.52
  165.7 4.5 %all-to-all-done.5 = bf16[4,1,128]{2,1,0:T(2,128)(2,1)S(1)} async-done(((bf16[4,1,128]{2,1,0:T(2,128)(2,1)}), bf16[4,1,128]{2,1,0:T(2,128)(2,1)S(1)}, u32[]{:S(2)}, u32[]{:S(2)}) %all-to-all-start.5) | async-done | bytes 1056 | tf_op jit(solution)/shard_map/all_to_all | solution.py:89
  170.2 3.4 %all-to-all-start.3 = ((bf16[4,192,128]{2,1,0:T(8,128)(2,1)}), bf16[4,192,128]{2,1,0:T(8,128)(2,1)S(1)}, u32[]{:S(2)}, u32[]{:S(2)}) async-start(bf16[4,192,128]{2,1,0:T(8,128)(2,1)} %copy.52), calls=%async_computation.3 | async-start | bytes 393216 | tf_op jit(solution)/shard_map/all_to_all | solution.py:87
  173.6 0.4 convolution_convert_fusion.2
  174.0 1.1 copy.84
  175.1 0.8 convolution_bitcast_fusion.1
  175.9 3.9 %all-to-all-done.3 = bf16[4,192,128]{2,1,0:T(8,128)(2,1)S(1)} async-done(((bf16[4,192,128]{2,1,0:T(8,128)(2,1)}), bf16[4,192,128]{2,1,0:T(8,128)(2,1)S(1)}, u32[]{:S(2)}, u32[]{:S(2)}) %all-to-all-start.3) | async-done | bytes 196640 | tf_op jit(solution)/shard_map/all_to_all | solution.py:87
  179.8 0.4 convolution_convert_fusion.3
  180.2 1.1 copy.85
  (20 shorter events, 0.0 us)
Async XLA Ops:
  7.2 1.8 copy-start
  7.2 11.8 %copy-start.2 = (bf16[192,2048]{1,0:T(8,128)(2,1)S(1)}, bf16[192,2048]{1,0:T(8,128)(2,1)}, u32[]{:S(2)}) copy-start(bf16[192,2048]{1,0:T(8,128)(2,1)} %param.10) | copy-start | bytes 2359300
  9.7 11.9 %all-to-all-start.1 = ((bf16[4,1,128]{2,1,0:T(2,128)(2,1)}), bf16[4,1,128]{2,1,0:T(2,128)(2,1)S(1)}, u32[]{:S(2)}, u32[]{:S(2)}) async-start(bf16[4,1,128]{2,1,0:T(2,128)(2,1)} %copy.46), calls=%async_computation.1 | async-start | bytes 4096 | tf_op jit(solution)/shard_map/all_to_all | solution.py:41
  16.7 2.8 %copy-start.10 = (pred[4]{0:T(512)(128)(4,1)}, pred[4]{0:T(512)(128)(4,1)S(1)}, u32[]{:S(2)}) copy-start(pred[4]{0:T(512)(128)(4,1)S(1)} %get-tuple-element.5) | copy-start | bytes 16
  16.7 78.4 %copy-start.8 = (f32[4]{0:T(128)}, f32[4]{0:T(128)S(1)}, u32[]{:S(2)}) copy-start(f32[4]{0:T(128)S(1)} %get-tuple-element.4) | copy-start | bytes 52
  17.4 1.8 copy-start.12
  17.4 78.0 %copy-start.6 = (bf16[4]{0:T(256)(128)(2,1)}, bf16[4]{0:T(256)(128)(2,1)S(1)}, u32[]{:S(2)}) copy-start(bf16[4]{0:T(256)(128)(2,1)S(1)} %get-tuple-element.10) | copy-start | bytes 28
  19.0 19.0 %copy-start.4 = (bf16[192,1024]{1,0:T(8,128)(2,1)S(1)}, bf16[192,1024]{1,0:T(8,128)(2,1)}, u32[]{:S(2)}) copy-start(bf16[192,1024]{1,0:T(8,128)(2,1)} %param.8) | copy-start | bytes 1179652
  21.6 12.4 %all-to-all-start = ((bf16[4,192,128]{2,1,0:T(8,128)(2,1)}), bf16[4,192,128]{2,1,0:T(8,128)(2,1)S(1)}, u32[]{:S(2)}, u32[]{:S(2)}) async-start(bf16[4,192,128]{2,1,0:T(8,128)(2,1)} %copy.45), calls=%async_computation | async-start | bytes 393216 | tf_op jit(solution)/shard_map/all_to_all | solution.py:39
  34.0 61.4 %all-to-all-start.2 = ((bf16[4,192,128]{2,1,0:T(8,128)(2,1)}), bf16[4,192,128]{2,1,0:T(8,128)(2,1)S(1)}, u32[]{:S(2)}, u32[]{:S(2)}) async-start(bf16[4,192,128]{2,1,0:T(8,128)(2,1)} %copy.47), calls=%async_computation.2 | async-start | bytes 393216 | tf_op jit(solution)/shard_map/all_to_all | solution.py:40
  37.3 119.6 %all-reduce.3.cloned.1.call-start = ((), (), s32[]{:S(2)}) async-start(), calls=%async_computation.6 | async-start | bytes 2097152 | tf_op jit(solution)/shard_map/psum | solution.py:68
  96.7 1.6 copy-start.3
  96.7 1.6 copy-start.7
  99.9 57.1 %copy-start.9 = (f32[4]{0:T(128)S(1)}, f32[4]{0:T(128)}, u32[]{:S(2)}) copy-start(f32[4]{0:T(128)} %copy-done.8) | copy-start | bytes 52
  100.4 58.5 %copy-start.11 = (pred[4]{0:T(512)(128)(4,1)S(1)}, pred[4]{0:T(512)(128)(4,1)}, u32[]{:S(2)}) copy-start(pred[4]{0:T(512)(128)(4,1)} %copy-done.10) | copy-start | bytes 16
  100.4 58.5 %copy-start.13 = (s32[4]{0:T(128)S(1)}, s32[4]{0:T(128)}, u32[]{:S(2)}) copy-start(s32[4]{0:T(128)} %copy-done.12) | copy-start | bytes 52
  102.1 58.1 %all-to-all-start.4 = ((bf16[4,192,128]{2,1,0:T(8,128)(2,1)}), bf16[4,192,128]{2,1,0:T(8,128)(2,1)S(1)}, u32[]{:S(2)}, u32[]{:S(2)}) async-start(bf16[4,192,128]{2,1,0:T(8,128)(2,1)} %copy.56), calls=%async_computation.4 | async-start | bytes 393216 | tf_op jit(solution)/shard_map/all_to_all | solution.py:88
  156.9 2.7 %copy-start.1 = (bf16[1024,4,128]{0,2,1:T(8,128)(2,1)S(1)}, bf16[1024,4,128]{0,2,1:T(8,128)(2,1)}, u32[]{:S(2)}) copy-start(bf16[1024,4,128]{0,2,1:T(8,128)(2,1)} %all-reduce.3.cloned.1.call-done) | copy-start | bytes 3145732
  156.9 2.7 %copy-start.5 = (bf16[192,1024]{1,0:T(8,128)(2,1)S(1)}, bf16[192,1024]{1,0:T(8,128)(2,1)}, u32[]{:S(2)}) copy-start(bf16[192,1024]{1,0:T(8,128)(2,1)} %param.8) | copy-start | bytes 1179652
  160.2 10.0 %all-to-all-start.5 = ((bf16[4,1,128]{2,1,0:T(2,128)(2,1)}), bf16[4,1,128]{2,1,0:T(2,128)(2,1)S(1)}, u32[]{:S(2)}, u32[]{:S(2)}) async-start(bf16[4,1,128]{2,1,0:T(2,128)(2,1)} %copy.58), calls=%async_computation.5 | async-start | bytes 4096 | tf_op jit(solution)/shard_map/all_to_all | solution.py:89
  170.2 9.6 %all-to-all-start.3 = ((bf16[4,192,128]{2,1,0:T(8,128)(2,1)}), bf16[4,192,128]{2,1,0:T(8,128)(2,1)S(1)}, u32[]{:S(2)}, u32[]{:S(2)}) async-start(bf16[4,192,128]{2,1,0:T(8,128)(2,1)} %copy.52), calls=%async_computation.3 | async-start | bytes 393216 | tf_op jit(solution)/shard_map/all_to_all | solution.py:87
Sparse Core Ops, SparseCore 0:
  100.0 56.8 all-reduce.2
where the time goes:
time: 189 us; the launch traced here: 188 us
  waiting for transfers between devices  65 us (34%)
  blocking collectives  56.5 us (30%)
  starting transfers between devices  27.7 us (15%)
  between operations  14.3 us (8%)
  local copies, waits for them, and re-layouts  10.1 us (5%)
  matrix products  8.36 us (4%)
  other arithmetic  6.22 us (3%)
    psum x1, blocking collectives, local(): preact = lax.psum(partial_value, 'layer') + bias_cols[None]  56.5 us
    psum x1, waiting for transfers between devices, local(): grad_total = lax.psum(back_part, 'layer')  49.9 us
    all_to_all x1, waiting for transfers between devices, local(): lax.all_to_all(enc_send, 'lat', split_axis=0, concat_axis=0, tiled=True)  6.63 us
    all_to_all x1, starting transfers between devices, local(): lax.all_to_all(bias_send, 'lat', split_axis=0, concat_axis=0, tiled=True)  6.35 us
    all_to_all x1, starting transfers between devices, local(): lax.all_to_all(enc_send, 'lat', split_axis=0, concat_axis=0, tiled=True)  5.09 us
    all_to_all x1, starting transfers between devices, local(): lax.all_to_all(dec_return, 'lat', split_axis=0, concat_axis=0, tiled=True)  4.97 us
    all_to_all x1, starting transfers between devices, local(): lax.all_to_all(bias_return, 'lat', split_axis=0, concat_axis=0, tiled=True)  4.55 us
    all_to_all x1, waiting for transfers between devices, local(): lax.all_to_all(bias_return, 'lat', split_axis=0, concat_axis=0, tiled=True)  4.53 us
  transfers between devices with their start and end apart: 7, of which 4 were waited for; matrix products, arithmetic and copies ran while one was open for 9% of the time, Pallas kernels for 0%

commit v1 on v0

--- a/solution.py
+++ b/solution.py
@@ -5,6 +5,20 @@
 from jax.sharding import PartitionSpec as P
 
 TILE = 128
+
+
+def balance_tables(base_x):
+    n_blocks = lax.axis_size("layer")
+
+    def shape_marks(outcome_arr, next_value):
+        if next_value >= n_blocks:
+            return outcome_arr
+        sides = []
+        for idx in [*range(n_blocks)]:
+            sides.append((idx, idx ^ next_value))
+        return shape_marks(outcome_arr + lax.ppermute(outcome_arr, "layer", sides), 2 * next_value)
+
+    return shape_marks(base_x, 1)
 
 
 def rounded(value):
@@ -65,7 +79,7 @@
     back_part = rounded(
         jnp.einsum("fr,kfc->rkc", grad_err, dec_cols, preferred_element_type=jnp.float32)
     )
-    grad_total = lax.psum(back_part, "layer")
+    grad_total = balance_tables(back_part)
     code_grad = (grad_total * (latent_codes > 0)).astype(jnp.bfloat16)
     enc_grad = jnp.einsum(
         "fr,rkc->kfc", activations, code_grad, preferred_element_type=jnp.float32

time: 189 us -> 224 us (1.19)
  waiting for transfers between devices: 65 us -> 106 us
  between operations: 14.3 us -> 0.99 us
  other arithmetic: 6.22 us -> 10.8 us
  starting transfers between devices: 27.7 us -> 31 us
    ppermute x0 -> x3, waiting for transfers between devices: none -> 90.4 us  [shape_marks(): lax.ppermute(outcome_arr, 'layer', sides)]
    psum x1 -> x0, waiting for transfers between devices: 49.9 us -> none  [local(): grad_total = lax.psum(back_part, 'layer')]
  transfers between devices with their start and end apart: 7 -> 9, of which waited for: 4 -> 6; matrix products, arithmetic and copies ran while one was open for 9% -> 8% of each run, Pallas kernels for 0% -> 0%
where the time goes in v1:
time: 224 us; the launch traced here: 223 us
  waiting for transfers between devices  106 us (47%)
  blocking collectives  56.5 us (25%)
  starting transfers between devices  31 us (14%)
  local copies, waits for them, and re-layouts  11.6 us (5%)
  other arithmetic  10.8 us (5%)
  matrix products  7.07 us (3%)
    ppermute x3, waiting for transfers between devices, shape_marks(): lax.ppermute(outcome_arr, 'layer', sides)  90.4 us
    psum x1, blocking collectives, local(): preact = lax.psum(partial_value, 'layer') + bias_cols[None]  56.5 us
    all_to_all x1, waiting for transfers between devices, local(): lax.all_to_all(enc_send, 'lat', split_axis=0, concat_axis=0, tiled=True)  6.62 us
    all_to_all x1, starting transfers between devices, local(): lax.all_to_all(bias_send, 'lat', split_axis=0, concat_axis=0, tiled=True)  6.35 us
    all_to_all x1, starting transfers between devices, local(): lax.all_to_all(enc_send, 'lat', split_axis=0, concat_axis=0, tiled=True)  5.09 us
    all_to_all x1, starting transfers between devices, local(): lax.all_to_all(bias_return, 'lat', split_axis=0, concat_axis=0, tiled=True)  5.02 us
    all_to_all x1, starting transfers between devices, local(): lax.all_to_all(dec_return, 'lat', split_axis=0, concat_axis=0, tiled=True)  4.96 us
    all_to_all x1, waiting for transfers between devices, local(): lax.all_to_all(bias_return, 'lat', split_axis=0, concat_axis=0, tiled=True)  4.53 us
  transfers between devices with their start and end apart: 9, of which 6 were waited for; matrix products, arithmetic and copies ran while one was open for 8% of the time, Pallas kernels for 0%

profile of v1, /device:TPU:0, one launch (start us, length us, event | category | flops | bytes accessed | tf_op | source)
XLA Modules:
  0.0 223.5 jit_solution(18399068732275928717)
XLA Ops:
  0.6 0.0 copy-start
  0.6 0.0 copy-start.2
  0.7 0.9 fusion.44
  1.5 0.8 fusion.23
  2.3 0.1 fusion.26
  2.4 0.0 copy-done
  2.4 0.1 fusion.8
  2.5 0.6 copy.46
  3.1 6.3 %all-to-all-start.1 = ((bf16[4,1,128]{2,1,0:T(2,128)(2,1)}), bf16[4,1,128]{2,1,0:T(2,128)(2,1)S(1)}, u32[]{:S(2)}, u32[]{:S(2)}) async-start(bf16[4,1,128]{2,1,0:T(2,128)(2,1)} %copy.46), calls=%async_computation.1 | async-start | bytes 4096 | tf_op jit(solution)/shard_map/all_to_all | solution.py:55
  9.5 1.3 fusion.42
  10.8 0.7 compare_and_fusion
  11.5 0.5 copy-done.10
  12.1 1.3 copy.65
  13.4 0.3 convolution_convert_fusion.7
  13.6 0.0 copy-start.1
  13.6 0.2 copy.66
  13.8 0.3 convolution_convert_fusion.6
  14.1 0.7 fusion.35
  14.8 0.7 copy.45
  15.5 0.7 copy.47
  16.2 0.0 all-to-all-done.1
  16.2 5.1 %all-to-all-start = ((bf16[4,192,128]{2,1,0:T(8,128)(2,1)}), bf16[4,192,128]{2,1,0:T(8,128)(2,1)S(1)}, u32[]{:S(2)}, u32[]{:S(2)}) async-start(bf16[4,192,128]{2,1,0:T(8,128)(2,1)} %copy.45), calls=%async_computation | async-start | bytes 393216 | tf_op jit(solution)/shard_map/all_to_all | solution.py:53
  21.3 0.6 gather_fusion
  21.9 0.1 select_convert_fusion.1
  21.9 6.6 %all-to-all-done = bf16[4,192,128]{2,1,0:T(8,128)(2,1)S(1)} async-done(((bf16[4,192,128]{2,1,0:T(8,128)(2,1)}), bf16[4,192,128]{2,1,0:T(8,128)(2,1)S(1)}, u32[]{:S(2)}, u32[]{:S(2)}) %all-to-all-start) | async-done | bytes 196640 | tf_op jit(solution)/shard_map/all_to_all | solution.py:53
  28.5 4.0 %all-to-all-start.2 = ((bf16[4,192,128]{2,1,0:T(8,128)(2,1)}), bf16[4,192,128]{2,1,0:T(8,128)(2,1)}, u32[]{:S(2)}, u32[]{:S(2)}) async-start(bf16[4,192,128]{2,1,0:T(8,128)(2,1)} %copy.47), calls=%async_computation.2 | async-start | bytes 393216 | tf_op jit(solution)/shard_map/all_to_all | solution.py:54
  32.5 0.0 copy-done.4
  32.6 0.6 gather_fusion.1
  33.2 0.6 fusion
  33.7 56.5 %all-reduce.1 = f32[1024,4,128]{0,2,1:T(8,128)S(1)} all-reduce(bf16[1024,4,128]{0,2,1:T(8,128)(2,1)S(1)} %fusion), channel_id=1, replica_groups=mesh['layer'=8,'lat'=4] {'layer'}, use_global_device_ids=true, to_apply=%region_2.4 | all-reduce | flops 524288 | bytes 3145728 | tf_op jit(solution)/shard_map/psum | solution.py:67
  90.3 1.0 multiply_convert_fusion
  91.3 0.0 all-to-all-done.2
  91.3 2.3 %gather_fusion.2 = bf16[4,192,128]{2,1,0:T(8,128)(2,1)} fusion(bf16[4,192,128]{2,1,0:T(8,128)(2,1)} %all-to-all-done.2, s32[1024]{0:T(1024)} %copy-done.4), kind=kCustom, calls=%fused_computation.1.clone | custom fusion | bytes 393232 | tf_op jit(solution)/shard_map/jit(_take)/gather | solution.py:69
  93.6 1.4 fusion.5
  95.0 1.2 convolution_convert_fusion
  96.2 0.2 convert_element_type.114
  96.5 0.1 collective-permute-start
  96.5 4.1 %collective-permute-done = f32[1024,4,128]{0,2,1:T(8,128)S(1)} collective-permute-done((f32[1024,4,128]{0,2,1:T(8,128)S(1)}, f32[1024,4,128]{0,2,1:T(8,128)S(1)}, u32[]{:S(2)}, u32[]{:S(2)}) %collective-permute-start) | collective-permute-done | bytes 2097184 | tf_op jit(solution)/shard_map/ppermute | solution.py:19
  100.7 0.4 convert_add_fusion
  101.1 0.9 collective-permute-start.1
  102.0 46.8 %collective-permute-done.1 = f32[1024,4,128]{0,2,1:T(8,128)S(1)} collective-permute-done((f32[1024,4,128]{0,2,1:T(8,128)S(1)}, f32[1024,4,128]{0,2,1:T(8,128)S(1)}, u32[]{:S(2)}, u32[]{:S(2)}) %collective-permute-start.1) | collective-permute-done | bytes 2097184 | tf_op jit(solution)/shard_map/ppermute | solution.py:19
  148.9 1.7 add.78
  150.6 1.2 collective-permute-start.2
  151.8 0.5 fusion.7
  152.4 0.3 convolution_convert_fusion.8
  152.6 0.7 copy.56
  153.3 5.0 %all-to-all-start.4 = ((bf16[4,192,128]{2,1,0:T(8,128)(2,1)}), bf16[4,192,128]{2,1,0:T(8,128)(2,1)S(1)}, u32[]{:S(2)}, u32[]{:S(2)}) async-start(bf16[4,192,128]{2,1,0:T(8,128)(2,1)} %copy.56), calls=%async_computation.4 | async-start | bytes 393216 | tf_op jit(solution)/shard_map/all_to_all | solution.py:102
  158.3 39.4 %collective-permute-done.2 = f32[1024,4,128]{0,2,1:T(8,128)} collective-permute-done((f32[1024,4,128]{0,2,1:T(8,128)}, f32[1024,4,128]{0,2,1:T(8,128)}, u32[]{:S(2)}, u32[]{:S(2)}) %collective-permute-start.2) | collective-permute-done | bytes 2097184 | tf_op jit(solution)/shard_map/ppermute | solution.py:19
  197.7 2.9 %fusion.41 = (bf16[4,128]{1,0:T(4,128)(2,1)S(1)}, bf16[1024,4,128]{0,2,1:T(8,128)(2,1)S(1)}) fusion(f32[1024,4,128]{0,2,1:T(8,128)} %add.78, f32[1024,4,128]{0,2,1:T(8,128)} %collective-permute-done.2, f32[4]{0:T(128)S(1)} %copy-done.5, f32[1024,4,128]{0,2,1:T(8,128)S(1)} %all-reduce.1, f32[4,128]{1,0:T(4,128)S(1)} %select_convert_fusion.1), kind=kLoop, calls=%fused_computation.91 | loop fusion | flops 4718080 | bytes 7343120 | tf_op jit(solution)/shard_map/reduce_sum | solution.py:87
  200.6 0.1 fusion.9
  200.8 0.6 copy.58
  201.3 0.5 fusion.6
  201.8 0.0 all-to-all-done.4
  201.9 5.0 %all-to-all-start.5 = ((bf16[4,1,128]{2,1,0:T(2,128)(2,1)}), bf16[4,1,128]{2,1,0:T(2,128)(2,1)S(1)}, u32[]{:S(2)}, u32[]{:S(2)}) async-start(bf16[4,1,128]{2,1,0:T(2,128)(2,1)} %copy.58), calls=%async_computation.5 | async-start | bytes 4096 | tf_op jit(solution)/shard_map/all_to_all | solution.py:103
  206.9 0.3 convolution_convert_fusion.9
  207.1 0.7 copy.52
  207.8 4.5 %all-to-all-done.5 = bf16[4,1,128]{2,1,0:T(2,128)(2,1)S(1)} async-done(((bf16[4,1,128]{2,1,0:T(2,128)(2,1)}), bf16[4,1,128]{2,1,0:T(2,128)(2,1)S(1)}, u32[]{:S(2)}, u32[]{:S(2)}) %all-to-all-start.5) | async-done | bytes 1056 | tf_op jit(solution)/shard_map/all_to_all | solution.py:103
  212.4 3.4 %all-to-all-start.3 = ((bf16[4,192,128]{2,1,0:T(8,128)(2,1)}), bf16[4,192,128]{2,1,0:T(8,128)(2,1)S(1)}, u32[]{:S(2)}, u32[]{:S(2)}) async-start(bf16[4,192,128]{2,1,0:T(8,128)(2,1)} %copy.52), calls=%async_computation.3 | async-start | bytes 393216 | tf_op jit(solution)/shard_map/all_to_all | solution.py:101
  215.7 0.4 convolution_convert_fusion.2
  216.2 1.1 copy.84
  217.3 0.8 convolution_bitcast_fusion.1
  218.0 3.9 %all-to-all-done.3 = bf16[4,192,128]{2,1,0:T(8,128)(2,1)S(1)} async-done(((bf16[4,192,128]{2,1,0:T(8,128)(2,1)}), bf16[4,192,128]{2,1,0:T(8,128)(2,1)S(1)}, u32[]{:S(2)}, u32[]{:S(2)}) %all-to-all-start.3) | async-done | bytes 196640 | tf_op jit(solution)/shard_map/all_to_all | solution.py:101
  222.0 0.4 convolution_convert_fusion.3
  222.4 1.1 copy.85
  (24 shorter events, 0.1 us)
Async XLA Ops:
  0.6 1.8 copy-start
  0.6 13.0 %copy-start.2 = (bf16[192,2048]{1,0:T(8,128)(2,1)S(1)}, bf16[192,2048]{1,0:T(8,128)(2,1)}, u32[]{:S(2)}) copy-start(bf16[192,2048]{1,0:T(8,128)(2,1)} %param.10) | copy-start | bytes 2359300
  3.1 13.0 %all-to-all-start.1 = ((bf16[4,1,128]{2,1,0:T(2,128)(2,1)}), bf16[4,1,128]{2,1,0:T(2,128)(2,1)S(1)}, u32[]{:S(2)}, u32[]{:S(2)}) async-start(bf16[4,1,128]{2,1,0:T(2,128)(2,1)} %copy.46), calls=%async_computation.1 | async-start | bytes 4096 | tf_op jit(solution)/shard_map/all_to_all | solution.py:55
  10.8 0.7 copy-start.7
  11.5 0.6 copy-start.10
  11.5 21.7 %copy-start.6 = (bf16[4]{0:T(256)(128)(2,1)}, bf16[4]{0:T(256)(128)(2,1)S(1)}, u32[]{:S(2)}) copy-start(bf16[4]{0:T(256)(128)(2,1)S(1)} %get-tuple-element.12) | copy-start | bytes 28
  12.1 20.5 %copy-start.4 = (s32[1024]{0:T(1024)}, s32[1024]{0:T(1024)S(1)}, u32[]{:S(2)}) copy-start(s32[1024]{0:T(1024)S(1)} %pad_clamp_fusion.1) | copy-start | bytes 12292
  13.6 19.5 %copy-start.1 = (bf16[192,1024]{1,0:T(8,128)(2,1)S(1)}, bf16[192,1024]{1,0:T(8,128)(2,1)}, u32[]{:S(2)}) copy-start(bf16[192,1024]{1,0:T(8,128)(2,1)} %param.8) | copy-start | bytes 1179652
  16.2 12.4 %all-to-all-start = ((bf16[4,192,128]{2,1,0:T(8,128)(2,1)}), bf16[4,192,128]{2,1,0:T(8,128)(2,1)S(1)}, u32[]{:S(2)}, u32[]{:S(2)}) async-start(bf16[4,192,128]{2,1,0:T(8,128)(2,1)} %copy.45), calls=%async_computation | async-start | bytes 393216 | tf_op jit(solution)/shard_map/all_to_all | solution.py:53
  28.5 62.7 %all-to-all-start.2 = ((bf16[4,192,128]{2,1,0:T(8,128)(2,1)}), bf16[4,192,128]{2,1,0:T(8,128)(2,1)}, u32[]{:S(2)}, u32[]{:S(2)}) async-start(bf16[4,192,128]{2,1,0:T(8,128)(2,1)} %copy.47), calls=%async_computation.2 | async-start | bytes 393216 | tf_op jit(solution)/shard_map/all_to_all | solution.py:54
  93.6 1.4 copy-start.3
  96.5 4.2 %collective-permute-start = (f32[1024,4,128]{0,2,1:T(8,128)S(1)}, f32[1024,4,128]{0,2,1:T(8,128)S(1)}, u32[]{:S(2)}, u32[]{:S(2)}) collective-permute-start(f32[1024,4,128]{0,2,1:T(8,128)S(1)} %convert_element_type.114), channel_id=1, source_target_pairs={{0,4},{4,0},{8,12},{12,8},{16,20},{20,16},{24,28},{28,24},{1,5},{5... | collective-permute-start | bytes 6291464 | tf_op jit(solution)/shard_map/ppermute | solution.py:19
  101.1 51.2 %copy-start.8 = (pred[4]{0:T(512)(128)(4,1)S(1)}, pred[4]{0:T(512)(128)(4,1)}, u32[]{:S(2)}) copy-start(pred[4]{0:T(512)(128)(4,1)} %copy-done.7) | copy-start | bytes 16
  101.1 51.2 %copy-start.11 = (s32[4]{0:T(128)S(1)}, s32[4]{0:T(128)}, u32[]{:S(2)}) copy-start(s32[4]{0:T(128)} %copy-done.10) | copy-start | bytes 52
  101.1 47.7 %collective-permute-start.1 = (f32[1024,4,128]{0,2,1:T(8,128)S(1)}, f32[1024,4,128]{0,2,1:T(8,128)S(1)}, u32[]{:S(2)}, u32[]{:S(2)}) collective-permute-start(f32[1024,4,128]{0,2,1:T(8,128)S(1)} %convert_add_fusion), channel_id=1, source_target_pairs={{0,8},{4,12},{8,0},{12,4},{16,24},{20,28},{24,16},{28,20},{1,9},{5... | collective-permute-start | bytes 6291464 | tf_op jit(solution)/shard_map/ppermute | solution.py:19
  150.6 47.1 %copy-start.5 = (f32[4]{0:T(128)S(1)}, f32[4]{0:T(128)}, u32[]{:S(2)}) copy-start(f32[4]{0:T(128)} %get-tuple-element.6) | copy-start | bytes 52
  150.6 47.1 %collective-permute-start.2 = (f32[1024,4,128]{0,2,1:T(8,128)}, f32[1024,4,128]{0,2,1:T(8,128)}, u32[]{:S(2)}, u32[]{:S(2)}) collective-permute-start(f32[1024,4,128]{0,2,1:T(8,128)} %add.78), channel_id=1, source_target_pairs={{0,16},{4,20},{8,24},{12,28},{16,0},{20,4},{24,8},{28,12},{1,17},{... | collective-permute-start | bytes 6291464 | tf_op jit(solution)/shard_map/ppermute | solution.py:19
  153.3 48.5 %all-to-all-start.4 = ((bf16[4,192,128]{2,1,0:T(8,128)(2,1)}), bf16[4,192,128]{2,1,0:T(8,128)(2,1)S(1)}, u32[]{:S(2)}, u32[]{:S(2)}) async-start(bf16[4,192,128]{2,1,0:T(8,128)(2,1)} %copy.56), calls=%async_computation.4 | async-start | bytes 393216 | tf_op jit(solution)/shard_map/all_to_all | solution.py:102
  158.3 42.3 %copy-start.9 = (pred[4]{0:T(512)(128)(4,1)S(1)}, pred[4]{0:T(512)(128)(4,1)}, u32[]{:S(2)}) copy-start(pred[4]{0:T(512)(128)(4,1)} %copy-done.7) | copy-start | bytes 16
  158.3 42.3 %copy-start.12 = (s32[4]{0:T(128)S(1)}, s32[4]{0:T(128)}, u32[]{:S(2)}) copy-start(s32[4]{0:T(128)} %copy-done.10) | copy-start | bytes 52
  201.9 10.5 %all-to-all-start.5 = ((bf16[4,1,128]{2,1,0:T(2,128)(2,1)}), bf16[4,1,128]{2,1,0:T(2,128)(2,1)S(1)}, u32[]{:S(2)}, u32[]{:S(2)}) async-start(bf16[4,1,128]{2,1,0:T(2,128)(2,1)} %copy.58), calls=%async_computation.5 | async-start | bytes 4096 | tf_op jit(solution)/shard_map/all_to_all | solution.py:103
  212.4 9.6 %all-to-all-start.3 = ((bf16[4,192,128]{2,1,0:T(8,128)(2,1)}), bf16[4,192,128]{2,1,0:T(8,128)(2,1)S(1)}, u32[]{:S(2)}, u32[]{:S(2)}) async-start(bf16[4,192,128]{2,1,0:T(8,128)(2,1)} %copy.52), calls=%async_computation.3 | async-start | bytes 393216 | tf_op jit(solution)/shard_map/all_to_all | solution.py:101
